TPU v7x, 256 devices: a whole 4x4x8 slice. The times are simulated.
256 devices in a mesh: group: 8 (over x, core), prompt: 32 (over z, y).
Axes of the slice: x: 4, y: 4, z: 8, core: 2. Of those that a mesh axis runs over, the one named last changes fastest.
Arguments:
- queries: bfloat16 [32, 8, 64, 3072], P('prompt', 'group'), may hold values from -48 to 48
- fresh_latent: bfloat16 [32, 8, 64, 576], P('prompt', 'group'), may hold values from -6 to 6
- latent_cache: bfloat16 [32, 8, 512, 576], P('prompt', 'group'), may hold values from -48 to 48
- selected: int32 [32, 8, 64], P('prompt', 'group'), may hold values from 0 to 511, as said below
- position: int32 [32, 8], P('prompt'), may hold values from 0 to 7, each once within a row
- latent_gain: bfloat16 [512], replicated, may hold values from 0.099609375 to 1.8984375
- kv_up: bfloat16 [512, 4096], P('prompt'), may hold values from -0.25 to 0.25
- out_weight: bfloat16 [2048, 2048], P('prompt'), may hold values from -0.125 to 0.125
Outputs:
- attended: bfloat16 [32, 8, 64, 2048], P('prompt', 'group')
- blended: bfloat16 [32, 8, 512, 576], P('prompt', 'group')
Inputs may be any that keep to these rules, and one draw needn't show every extreme that they name: `selected`: the 64 indices of a group are distinct and increasing.
All inputs are finite; a program needn't handle non-finite values.
Results may differ from a plain program's by a relative error of at most 0.011.
Values may be sent and summed in bfloat16 or wider, within the bound.
A program may use at most 128 MiB of HBM per device.

v0:
```python
import jax
import jax.numpy as jnp
from jax import lax
from jax.sharding import Mesh
from jax.sharding import PartitionSpec as P

D = 2048
H = 16
DN = 128
DR = 64
DV = 128
LAT = 512
PROMPT = ("prompt_0", "prompt_1")


def whole_of(array, axes, dim):
    whole = array
    for number in range(len(axes) - 1, -1, -1):
        whole = lax.all_gather(whole, axes[number], axis=dim, tiled=True)
    return whole


def rope_rotate(values, places):
    half = values.shape[-1] // 2
    freqs = 10000.0 ** (-jnp.arange(half, dtype=jnp.float32) / half)
    angles = places[..., None] * freqs
    cosine = jnp.cos(angles)
    sine = jnp.sin(angles)
    first = values[..., :half]
    second = values[..., half:]
    return jnp.concatenate([first * cosine - second * sine, second * cosine + first * sine], -1)


def prepare_rows(fresh, gain, places):
    latent = fresh[..., :LAT].astype(jnp.float32)
    factor = lax.rsqrt(jnp.mean(latent * latent, -1, keepdims=True) + 1e-06)
    normed = latent * factor * gain.astype(jnp.float32)
    turned = rope_rotate(fresh[..., LAT:].astype(jnp.float32), places)
    return jnp.concatenate([normed, turned], -1).astype(jnp.bfloat16)


def shards(queries, fresh_latent, latent_cache, selected, position, latent_gain, kv_up, out_weight):
    prompts, groups, picks, _ = queries.shape
    length = latent_cache.shape[2]
    first_group = lax.axis_index("group") * groups
    own_order = lax.dynamic_slice_in_dim(position, first_group, groups, 1)
    place_int = own_order[:, :, None] * length + selected
    places = place_int.astype(jnp.float32)
    fresh_rows = prepare_rows(fresh_latent, latent_gain, places)
    prompt_ids = jnp.arange(prompts, dtype=jnp.int32)[:, None, None]
    group_ids = jnp.arange(groups, dtype=jnp.int32)[None, :, None]
    blended = latent_cache.at[prompt_ids, group_ids, selected].set(fresh_rows)
    whole_kv = whole_of(kv_up, PROMPT, 0).reshape(LAT, H, DN + DV)
    shaped = queries.reshape(prompts, groups, picks, H, DN + DR)
    absorbed = jnp.einsum(
        "pcshd,lhd->pcshl", shaped[..., :DN], whole_kv[..., :DN], preferred_element_type=jnp.float32
    ).astype(jnp.bfloat16)
    turned = rope_rotate(shaped[..., DN:].astype(jnp.float32), places[..., None]).astype(
        jnp.bfloat16
    )
    rows = groups * picks
    query_vec = jnp.concatenate([absorbed, turned], -1).reshape(prompts, rows, H, LAT + DR)
    query_place = place_int.reshape(prompts, rows)
    scale = (DN + DR) ** (-0.5)
    offsets = jnp.arange(length, dtype=jnp.int32)

    def update(state, keys, key_place):
        peak, total, mixed = state
        allowed = (key_place[:, None, :] <= query_place[:, :, None])[:, :, None, :]
        scores = (
            jnp.einsum("pqhe,pke->pqhk", query_vec, keys, preferred_element_type=jnp.float32)
            * scale
        )
        block_peak = jnp.max(jnp.where(allowed, scores, -1e30), -1)
        new_peak = jnp.maximum(peak, block_peak)
        probs = jnp.where(allowed, jnp.exp(scores - new_peak[..., None]), 0.0)
        decay = jnp.exp(peak - new_peak)
        total = total * decay + jnp.sum(probs, -1)
        mixed = mixed * decay[..., None] + jnp.einsum(
            "pqhk,pkl->pqhl",
            probs.astype(jnp.bfloat16),
            keys[..., :LAT],
            preferred_element_type=jnp.float32,
        )
        return (new_peak, total, mixed)

    start_state = (
        jnp.full((prompts, rows, H), -1e30, jnp.float32),
        jnp.zeros((prompts, rows, H), jnp.float32),
        jnp.zeros((prompts, rows, H, LAT), jnp.float32),
    )
    piece = lax.all_gather(blended, "group", axis=1, tiled=True)

    def one_group(index, carry):
        keys = lax.dynamic_slice_in_dim(piece, index, 1, 1)[:, 0]
        order = lax.dynamic_slice_in_dim(position, index, 1, 1)
        key_place = order * length + offsets[None, :]
        needed = jnp.any(key_place[:, :1] <= jnp.max(query_place, -1, keepdims=True))
        return lax.cond(needed, lambda c: update(c, keys, key_place), lambda c: c, carry)

    peak, total, mixed = lax.fori_loop(0, piece.shape[1], one_group, start_state)
    latent_mix = (mixed / total[..., None]).astype(jnp.bfloat16)
    heads = jnp.einsum(
        "pqhl,lhv->pqhv", latent_mix, whole_kv[..., DN:], preferred_element_type=jnp.float32
    ).astype(jnp.bfloat16)
    heads = heads.reshape(prompts * rows, H * DV)
    whole_out = lax.all_gather(out_weight, PROMPT, axis=0, tiled=True)
    attended = jnp.dot(heads, whole_out, preferred_element_type=jnp.float32)
    return (attended.astype(jnp.bfloat16).reshape(prompts, groups, picks, D), blended)


def solution(mesh):
    split = Mesh(mesh.devices.reshape(mesh.shape["group"], 8, 4), ("group", "prompt_0", "prompt_1"))
    return jax.shard_map(
        shards,
        mesh=split,
        in_specs=(
            P(PROMPT, "group", None, None),
            P(PROMPT, "group", None, None),
            P(PROMPT, "group", None, None),
            P(PROMPT, "group", None),
            P(PROMPT, None),
            P(),
            P(PROMPT, None),
            P(PROMPT, None),
        ),
        out_specs=(P(PROMPT, "group", None, None), P(PROMPT, "group", None, None)),
        check_vma=False,
    )
```

profile of v0, /device:TPU:57, one launch (start us, length us, event | category | flops | bytes accessed | tf_op | source)
XLA Modules:
  0.0 239.9 jit_solution(15318648085517091847)
XLA Ops:
  7.2 10.8 %all_gather.13 = bf16[64,4096]{1,0:T(8,128)(2,1)} all-gather(bf16[16,4096]{1,0:T(8,128)(2,1)} %param.18), channel_id=1, replica_groups=mesh['group'=8,'prompt_0'=8,'prompt_1'=4] {'prompt_1'}, dimensions={0}, use_global_device_ids=true | all-gather | bytes 655360 | tf_op jit(solution)/shard_map/all_gather | solution.py:19
  29.4 46.8 %all-gather.5.cloned.1.call-done = bf16[512,4096]{1,0:T(8,128)(2,1)} async-done(((bf16[64,4096]{1,0:T(8,128)(2,1)}), bf16[512,4096]{1,0:T(8,128)(2,1)}) %all-gather.5.cloned.1.call-update) | async-done | bytes 4194320 | tf_op jit(solution)/shard_map/all_gather | solution.py:19
  76.2 6.5 %copy.53 = bf16[512,4096]{0,1:T(8,128)(2,1)} copy(bf16[512,4096]{1,0:T(8,128)(2,1)} %all-gather.5.cloned.1.call-done) | data formatting | bytes 8388608 | tf_op jit(solution)/shard_map/all_gather | solution.py:19
  86.1 31.9 %all-gather.9.cloned.1.call-done = bf16[4096,576]{1,0:T(8,128)(2,1)} async-done(((bf16[512,576]{1,0:T(8,128)(2,1)}), bf16[4096,576]{1,0:T(8,128)(2,1)}) %all-gather.9.cloned.1.call-update) | async-done | bytes 4718608 | tf_op jit(solution)/shard_map/all_gather | solution.py:92
  118.0 7.7 %copy.57 = bf16[1,8,512,576]{2,3,1,0:T(8,128)(2,1)} copy(bf16[1,8,512,576]{3,2,1,0:T(8,128)(2,1)} %bitcast.103) | data formatting | bytes 9437184
  126.3 98.4 %while.20 = (s32[]{:T(128)}, f32[1,64,16]{1,2,0:T(8,128)S(1)}, f32[1,64,16]{1,2,0:T(8,128)S(1)}, f32[1,64,16,512]{3,2,1,0:T(8,128)S(1)}, s32[1,8]{1,0:T(1,128)S(...) while((s32[]{:T(128)}, f32[1,64,16]{1,2,0:T(8,128)S(1)}, ...), condition=%wide.region_8.9_spmd.clone, body=%wide.region_3.8_spmd.clone.sunk | while | flops 1146129920 | bytes 17670692 | solution.py:101
  129.5 9.0 %conditional.3 = ((f32[1,64,16]{1,2,0:T(8,128)S(1)}, f32[1,64,16]{1,2,0:T(8,128)S(1)}, f32[1,64,16,512]{3,2,1,0:T(8,128)S(1)})) conditional(s32[]{:T(128)} %bitcast.97, (f32[1,64,16]{1,2,0:T(8,128)S(1)}, f32[1,64,16]{1,2,0:T(8,128)S(1)}, f32[1,64,16,512]{3,2,1,0:T(8,128)S(1)}) %tuple.70, (s32[1,512]{1,0:T(1,128)S(1)}, s32[1,1,64]{2,1,0:T(1,128)S(1)}, ...), branch_computations={%region_4.0_spmd, %region_5.7_spmd} | conditional | flops 1146129408 | bytes 17668416 | solution.py:99
  130.8 2.5 %fusion.2 = (f32[64,16]{0,1:T(8,128)S(1)}, f32[512,64,16]{0,1,2:T(8,128)S(1)}) fusion(pred[64,512]{1,0:T(8,128)(4,1)S(1)} %broadcast_compare_fusion, bf16[1,64,16,576]{3,1,2,0:T(8,128)(2,1)} %get-tuple-element.279, bf16[1,1,512,576]{2,3,1,0:T(8,128)(2,1)S(1)} %constant_dynamic-slice_fusion), kind=kOutput, calls=%fused_computation.5 | convolution fusion | flops 605551616 | bytes 3903488 | tf_op jit(solution)/shard_map/while/body/eval_jaxpr/cond/branch_1_fun/pqhe,pke->pqhk/dot_general | solution.py:71
  136.3 2.2 bitcast_add_fusion
  141.8 9.1 %conditional.3 = ((f32[1,64,16]{1,2,0:T(8,128)S(1)}, f32[1,64,16]{1,2,0:T(8,128)S(1)}, f32[1,64,16,512]{3,2,1,0:T(8,128)S(1)})) conditional(s32[]{:T(128)} %bitcast.97, (f32[1,64,16]{1,2,0:T(8,128)S(1)}, f32[1,64,16]{1,2,0:T(8,128)S(1)}, f32[1,64,16,512]{3,2,1,0:T(8,128)S(1)}) %tuple.70, (s32[1,512]{1,0:T(1,128)S(1)}, s32[1,1,64]{2,1,0:T(1,128)S(1)}, ...), branch_computations={%region_4.0_spmd, %region_5.7_spmd} | conditional | flops 1146129408 | bytes 17668416 | solution.py:99
  143.1 2.5 %fusion.2 = (f32[64,16]{0,1:T(8,128)S(1)}, f32[512,64,16]{0,1,2:T(8,128)S(1)}) fusion(pred[64,512]{1,0:T(8,128)(4,1)S(1)} %broadcast_compare_fusion, bf16[1,64,16,576]{3,1,2,0:T(8,128)(2,1)} %get-tuple-element.279, bf16[1,1,512,576]{2,3,1,0:T(8,128)(2,1)S(1)} %constant_dynamic-slice_fusion), kind=kOutput, calls=%fused_computation.5 | convolution fusion | flops 605551616 | bytes 3903488 | tf_op jit(solution)/shard_map/while/body/eval_jaxpr/cond/branch_1_fun/pqhe,pke->pqhk/dot_general | solution.py:71
  154.1 9.0 %conditional.3 = ((f32[1,64,16]{1,2,0:T(8,128)S(1)}, f32[1,64,16]{1,2,0:T(8,128)S(1)}, f32[1,64,16,512]{3,2,1,0:T(8,128)S(1)})) conditional(s32[]{:T(128)} %bitcast.97, (f32[1,64,16]{1,2,0:T(8,128)S(1)}, f32[1,64,16]{1,2,0:T(8,128)S(1)}, f32[1,64,16,512]{3,2,1,0:T(8,128)S(1)}) %tuple.70, (s32[1,512]{1,0:T(1,128)S(1)}, s32[1,1,64]{2,1,0:T(1,128)S(1)}, ...), branch_computations={%region_4.0_spmd, %region_5.7_spmd} | conditional | flops 1146129408 | bytes 17668416 | solution.py:99
  155.4 2.5 %fusion.2 = (f32[64,16]{0,1:T(8,128)S(1)}, f32[512,64,16]{0,1,2:T(8,128)S(1)}) fusion(pred[64,512]{1,0:T(8,128)(4,1)S(1)} %broadcast_compare_fusion, bf16[1,64,16,576]{3,1,2,0:T(8,128)(2,1)} %get-tuple-element.279, bf16[1,1,512,576]{2,3,1,0:T(8,128)(2,1)S(1)} %constant_dynamic-slice_fusion), kind=kOutput, calls=%fused_computation.5 | convolution fusion | flops 605551616 | bytes 3903488 | tf_op jit(solution)/shard_map/while/body/eval_jaxpr/cond/branch_1_fun/pqhe,pke->pqhk/dot_general | solution.py:71
  160.9 2.2 bitcast_add_fusion
  166.4 9.2 %conditional.3 = ((f32[1,64,16]{1,2,0:T(8,128)S(1)}, f32[1,64,16]{1,2,0:T(8,128)S(1)}, f32[1,64,16,512]{3,2,1,0:T(8,128)S(1)})) conditional(s32[]{:T(128)} %bitcast.97, (f32[1,64,16]{1,2,0:T(8,128)S(1)}, f32[1,64,16]{1,2,0:T(8,128)S(1)}, f32[1,64,16,512]{3,2,1,0:T(8,128)S(1)}) %tuple.70, (s32[1,512]{1,0:T(1,128)S(1)}, s32[1,1,64]{2,1,0:T(1,128)S(1)}, ...), branch_computations={%region_4.0_spmd, %region_5.7_spmd} | conditional | flops 1146129408 | bytes 17668416 | solution.py:99
  167.6 2.5 %fusion.2 = (f32[64,16]{0,1:T(8,128)S(1)}, f32[512,64,16]{0,1,2:T(8,128)S(1)}) fusion(pred[64,512]{1,0:T(8,128)(4,1)S(1)} %broadcast_compare_fusion, bf16[1,64,16,576]{3,1,2,0:T(8,128)(2,1)} %get-tuple-element.279, bf16[1,1,512,576]{2,3,1,0:T(8,128)(2,1)S(1)} %constant_dynamic-slice_fusion), kind=kOutput, calls=%fused_computation.5 | convolution fusion | flops 605551616 | bytes 3903488 | tf_op jit(solution)/shard_map/while/body/eval_jaxpr/cond/branch_1_fun/pqhe,pke->pqhk/dot_general | solution.py:71
  171.0 2.3 copy.47
  173.3 2.2 bitcast_add_fusion
  178.8 9.1 %conditional.3 = ((f32[1,64,16]{1,2,0:T(8,128)S(1)}, f32[1,64,16]{1,2,0:T(8,128)S(1)}, f32[1,64,16,512]{3,2,1,0:T(8,128)S(1)})) conditional(s32[]{:T(128)} %bitcast.97, (f32[1,64,16]{1,2,0:T(8,128)S(1)}, f32[1,64,16]{1,2,0:T(8,128)S(1)}, f32[1,64,16,512]{3,2,1,0:T(8,128)S(1)}) %tuple.70, (s32[1,512]{1,0:T(1,128)S(1)}, s32[1,1,64]{2,1,0:T(1,128)S(1)}, ...), branch_computations={%region_4.0_spmd, %region_5.7_spmd} | conditional | flops 1146129408 | bytes 17668416 | solution.py:99
  180.0 2.5 %fusion.2 = (f32[64,16]{0,1:T(8,128)S(1)}, f32[512,64,16]{0,1,2:T(8,128)S(1)}) fusion(pred[64,512]{1,0:T(8,128)(4,1)S(1)} %broadcast_compare_fusion, bf16[1,64,16,576]{3,1,2,0:T(8,128)(2,1)} %get-tuple-element.279, bf16[1,1,512,576]{2,3,1,0:T(8,128)(2,1)S(1)} %constant_dynamic-slice_fusion), kind=kOutput, calls=%fused_computation.5 | convolution fusion | flops 605551616 | bytes 3903488 | tf_op jit(solution)/shard_map/while/body/eval_jaxpr/cond/branch_1_fun/pqhe,pke->pqhk/dot_general | solution.py:71
  183.4 2.2 copy.47
  185.6 2.2 bitcast_add_fusion
  191.1 9.1 %conditional.3 = ((f32[1,64,16]{1,2,0:T(8,128)S(1)}, f32[1,64,16]{1,2,0:T(8,128)S(1)}, f32[1,64,16,512]{3,2,1,0:T(8,128)S(1)})) conditional(s32[]{:T(128)} %bitcast.97, (f32[1,64,16]{1,2,0:T(8,128)S(1)}, f32[1,64,16]{1,2,0:T(8,128)S(1)}, f32[1,64,16,512]{3,2,1,0:T(8,128)S(1)}) %tuple.70, (s32[1,512]{1,0:T(1,128)S(1)}, s32[1,1,64]{2,1,0:T(1,128)S(1)}, ...), branch_computations={%region_4.0_spmd, %region_5.7_spmd} | conditional | flops 1146129408 | bytes 17668416 | solution.py:99
  192.3 2.6 %fusion.2 = (f32[64,16]{0,1:T(8,128)S(1)}, f32[512,64,16]{0,1,2:T(8,128)S(1)}) fusion(pred[64,512]{1,0:T(8,128)(4,1)S(1)} %broadcast_compare_fusion, bf16[1,64,16,576]{3,1,2,0:T(8,128)(2,1)} %get-tuple-element.279, bf16[1,1,512,576]{2,3,1,0:T(8,128)(2,1)S(1)} %constant_dynamic-slice_fusion), kind=kOutput, calls=%fused_computation.5 | convolution fusion | flops 605551616 | bytes 3903488 | tf_op jit(solution)/shard_map/while/body/eval_jaxpr/cond/branch_1_fun/pqhe,pke->pqhk/dot_general | solution.py:71
  195.7 2.2 copy.47
  203.4 9.1 %conditional.3 = ((f32[1,64,16]{1,2,0:T(8,128)S(1)}, f32[1,64,16]{1,2,0:T(8,128)S(1)}, f32[1,64,16,512]{3,2,1,0:T(8,128)S(1)})) conditional(s32[]{:T(128)} %bitcast.97, (f32[1,64,16]{1,2,0:T(8,128)S(1)}, f32[1,64,16]{1,2,0:T(8,128)S(1)}, f32[1,64,16,512]{3,2,1,0:T(8,128)S(1)}) %tuple.70, (s32[1,512]{1,0:T(1,128)S(1)}, s32[1,1,64]{2,1,0:T(1,128)S(1)}, ...), branch_computations={%region_4.0_spmd, %region_5.7_spmd} | conditional | flops 1146129408 | bytes 17668416 | solution.py:99
  204.7 2.5 %fusion.2 = (f32[64,16]{0,1:T(8,128)S(1)}, f32[512,64,16]{0,1,2:T(8,128)S(1)}) fusion(pred[64,512]{1,0:T(8,128)(4,1)S(1)} %broadcast_compare_fusion, bf16[1,64,16,576]{3,1,2,0:T(8,128)(2,1)} %get-tuple-element.279, bf16[1,1,512,576]{2,3,1,0:T(8,128)(2,1)S(1)} %constant_dynamic-slice_fusion), kind=kOutput, calls=%fused_computation.5 | convolution fusion | flops 605551616 | bytes 3903488 | tf_op jit(solution)/shard_map/while/body/eval_jaxpr/cond/branch_1_fun/pqhe,pke->pqhk/dot_general | solution.py:71
  210.2 2.2 bitcast_add_fusion
  215.7 9.0 %conditional.3 = ((f32[1,64,16]{1,2,0:T(8,128)S(1)}, f32[1,64,16]{1,2,0:T(8,128)S(1)}, f32[1,64,16,512]{3,2,1,0:T(8,128)S(1)})) conditional(s32[]{:T(128)} %bitcast.97, (f32[1,64,16]{1,2,0:T(8,128)S(1)}, f32[1,64,16]{1,2,0:T(8,128)S(1)}, f32[1,64,16,512]{3,2,1,0:T(8,128)S(1)}) %tuple.70, (s32[1,512]{1,0:T(1,128)S(1)}, s32[1,1,64]{2,1,0:T(1,128)S(1)}, ...), branch_computations={%region_4.0_spmd, %region_5.7_spmd} | conditional | flops 1146129408 | bytes 17668416 | solution.py:99
  216.9 2.5 %fusion.2 = (f32[64,16]{0,1:T(8,128)S(1)}, f32[512,64,16]{0,1,2:T(8,128)S(1)}) fusion(pred[64,512]{1,0:T(8,128)(4,1)S(1)} %broadcast_compare_fusion, bf16[1,64,16,576]{3,1,2,0:T(8,128)(2,1)} %get-tuple-element.279, bf16[1,1,512,576]{2,3,1,0:T(8,128)(2,1)S(1)} %constant_dynamic-slice_fusion), kind=kOutput, calls=%fused_computation.5 | convolution fusion | flops 605551616 | bytes 3903488 | tf_op jit(solution)/shard_map/while/body/eval_jaxpr/cond/branch_1_fun/pqhe,pke->pqhk/dot_general | solution.py:71
  225.1 2.4 %fusion.26 = bf16[1,64,16,128]{3,1,2,0:T(8,128)(2,1)S(1)} fusion(bf16[512,16,256]{0,2,1:T(8,128)(2,1)} %bitcast.100, bf16[64,16,512]{2,1,0:T(8,128)(2,1)S(1)} %fusion.30), kind=kOutput, calls=%fused_computation.34 | convolution fusion | flops 134348800 | bytes 3407872 | tf_op jit(solution)/shard_map/pqhl,lhv->pqhv/dot_general | solution.py:103
  227.7 5.7 %fusion.12 = bf16[1,1,64,2048]{3,2,1,0:T(8,128)(2,1)} fusion(bf16[2048,2048]{1,0:T(8,128)(2,1)} %all-gather.7.cloned.1.call-done, bf16[8,8,16,128]{3,2,1,0:T(8,128)(2,1)S(1)} %bitcast.105), kind=kOutput, calls=%fused_computation.24 | convolution fusion | flops 537001984 | bytes 8912896 | tf_op jit(solution)/shard_map/dot_general | solution.py:108
  (159 shorter events, 65.1 us)
Async XLA Ops:
  7.2 16.2 %copy-start.5 = (bf16[1,1,64,576]{3,2,1,0:T(8,128)(2,1)S(1)}, bf16[1,1,64,576]{3,2,1,0:T(8,128)(2,1)}, u32[]{:S(2)}) copy-start(bf16[1,1,64,576]{3,2,1,0:T(8,128)(2,1)} %param.13) | copy-start | bytes 221188
  7.2 16.1 %copy-start.6 = (bf16[512]{0:T(512)(128)(2,1)S(1)}, bf16[512]{0:T(512)(128)(2,1)}, u32[]{:S(2)}) copy-start(bf16[512]{0:T(512)(128)(2,1)} %param.17) | copy-start | bytes 3076
  7.2 69.0 %all-gather.5.cloned.1.call-start = ((), (), s32[]{:S(2)}) async-start(), calls=%async_computation | async-start | bytes 4718592 | tf_op jit(solution)/shard_map/all_gather | solution.py:19
  18.1 8.4 %copy-start.4 = (bf16[1,1,64,3072]{3,2,1,0:T(8,128)(2,1)S(1)}, bf16[1,1,64,3072]{3,2,1,0:T(8,128)(2,1)}, u32[]{:S(2)}) copy-start(bf16[1,1,64,3072]{3,2,1,0:T(8,128)(2,1)} %param.12) | copy-start | bytes 1179652
  18.1 99.9 %all-gather.9.cloned.1.call-start = ((), (), s32[]{:S(2)}) async-start(), calls=%async_computation.2 | async-start | bytes 5898240 | tf_op jit(solution)/shard_map/all_gather | solution.py:92
  24.9 0.8 copy-start.1
  25.8 1.4 copy-start.2
  25.8 201.9 %all-gather.7.cloned.1.call-start = ((), (), s32[]{:S(2)}) async-start(), calls=%async_computation.1 | async-start | bytes 8650752 | tf_op jit(solution)/shard_map/all_gather | solution.py:107
  27.1 2.3 copy-start.3
  76.2 6.5 %slice-start = ((bf16[1,1,64,16,192]{4,3,2,1,0:T(8,128)(2,1)}), bf16[1,1,64,16,128]{4,3,2,1,0:T(8,128)(2,1)S(1)}, s32[]{:S(2)}) async-start(bf16[1,1,64,16,192]{4,3,2,1,0:T(8,128)(2,1)} %copy-done.3), calls=%async_computation.3 | async-start | bytes 524288 | tf_op jit(solution)/shard_map/slice | solution.py:56
  125.7 0.7 copy-start.7
  130.7 2.6 %copy-start = (bf16[1,1,512,576]{2,3,1,0:T(8,128)(2,1)}, bf16[1,1,512,576]{2,3,1,0:T(8,128)(2,1)S(1)}, u32[]{:S(2)}) copy-start(bf16[1,1,512,576]{2,3,1,0:T(8,128)(2,1)S(1)} %constant_dynamic-slice_fusion) | copy-start | bytes 1769476 | tf_op jit(solution)/shard_map/while/body/eval_jaxpr/cond
  143.0 2.7 %copy-start = (bf16[1,1,512,576]{2,3,1,0:T(8,128)(2,1)}, bf16[1,1,512,576]{2,3,1,0:T(8,128)(2,1)S(1)}, u32[]{:S(2)}) copy-start(bf16[1,1,512,576]{2,3,1,0:T(8,128)(2,1)S(1)} %constant_dynamic-slice_fusion) | copy-start | bytes 1769476 | tf_op jit(solution)/shard_map/while/body/eval_jaxpr/cond
  155.3 2.6 %copy-start = (bf16[1,1,512,576]{2,3,1,0:T(8,128)(2,1)}, bf16[1,1,512,576]{2,3,1,0:T(8,128)(2,1)S(1)}, u32[]{:S(2)}) copy-start(bf16[1,1,512,576]{2,3,1,0:T(8,128)(2,1)S(1)} %constant_dynamic-slice_fusion) | copy-start | bytes 1769476 | tf_op jit(solution)/shard_map/while/body/eval_jaxpr/cond
  167.5 2.6 %copy-start = (bf16[1,1,512,576]{2,3,1,0:T(8,128)(2,1)}, bf16[1,1,512,576]{2,3,1,0:T(8,128)(2,1)S(1)}, u32[]{:S(2)}) copy-start(bf16[1,1,512,576]{2,3,1,0:T(8,128)(2,1)S(1)} %constant_dynamic-slice_fusion) | copy-start | bytes 1769476 | tf_op jit(solution)/shard_map/while/body/eval_jaxpr/cond
  179.9 2.6 %copy-start = (bf16[1,1,512,576]{2,3,1,0:T(8,128)(2,1)}, bf16[1,1,512,576]{2,3,1,0:T(8,128)(2,1)S(1)}, u32[]{:S(2)}) copy-start(bf16[1,1,512,576]{2,3,1,0:T(8,128)(2,1)S(1)} %constant_dynamic-slice_fusion) | copy-start | bytes 1769476 | tf_op jit(solution)/shard_map/while/body/eval_jaxpr/cond
  192.2 2.7 %copy-start = (bf16[1,1,512,576]{2,3,1,0:T(8,128)(2,1)}, bf16[1,1,512,576]{2,3,1,0:T(8,128)(2,1)S(1)}, u32[]{:S(2)}) copy-start(bf16[1,1,512,576]{2,3,1,0:T(8,128)(2,1)S(1)} %constant_dynamic-slice_fusion) | copy-start | bytes 1769476 | tf_op jit(solution)/shard_map/while/body/eval_jaxpr/cond
  204.6 2.6 %copy-start = (bf16[1,1,512,576]{2,3,1,0:T(8,128)(2,1)}, bf16[1,1,512,576]{2,3,1,0:T(8,128)(2,1)S(1)}, u32[]{:S(2)}) copy-start(bf16[1,1,512,576]{2,3,1,0:T(8,128)(2,1)S(1)} %constant_dynamic-slice_fusion) | copy-start | bytes 1769476 | tf_op jit(solution)/shard_map/while/body/eval_jaxpr/cond
  216.8 2.6 %copy-start = (bf16[1,1,512,576]{2,3,1,0:T(8,128)(2,1)}, bf16[1,1,512,576]{2,3,1,0:T(8,128)(2,1)S(1)}, u32[]{:S(2)}) copy-start(bf16[1,1,512,576]{2,3,1,0:T(8,128)(2,1)S(1)} %constant_dynamic-slice_fusion) | copy-start | bytes 1769476 | tf_op jit(solution)/shard_map/while/body/eval_jaxpr/cond
Sparse Core Ops, SparseCore 0:
  18.2 57.9 all-gather.4
  78.0 39.9 all-gather.8
  120.6 93.4 all-gather.6
where the time goes:
time: 242 us; the launch traced here: 240 us
  waiting for transfers between devices  79.4 us (33%)
  local copies, waits for them, and re-layouts  52.4 us (22%)
  matrix products  48.2 us (20%)
  other arithmetic  24.2 us (10%)
  between operations  14 us (6%)
  blocking collectives  10.8 us (4%)
  loops' own time  10.8 us (4%)
    all_gather x1, waiting for transfers between devices, whole_of(): whole = lax.all_gather(whole, axes[number], axis=dim, tiled=True)  46.8 us
    all_gather x1, waiting for transfers between devices, shards(): piece = lax.all_gather(blended, 'group', axis=1, tiled=True)  31.9 us
    dynamic_slice x16, local copies, waits for them, and re-layouts, one_group(): keys = lax.dynamic_slice_in_dim(piece, index, 1, 1)[:, 0]  26.8 us
    dot_general x8, matrix products, update(): jnp.einsum('pqhe,pke->pqhk', query_vec, keys, preferred_element_type=jnp....  20.2 us
    dot_general x8, matrix products, update(): jnp.einsum('pqhk,pkl->pqhl', probs.astype(jnp.bfloat16), keys[..., :LAT],...  17.9 us
    unnamed x18, local copies, waits for them, and re-layouts  11.4 us
    all_gather x1, blocking collectives, whole_of(): whole = lax.all_gather(whole, axes[number], axis=dim, tiled=True)  10.8 us
    another operation x1, loops' own time, shards(): lax.fori_loop(0, piece.shape[1], one_group, start_state)  10.2 us
  transfers between devices with their start and end apart: 3, of which 2 were waited for; matrix products, arithmetic and copies ran while one was open for 49% of the time, Pallas kernels for 0%

commit v1 on v0

--- a/solution.py
+++ b/solution.py
@@ -89,7 +89,9 @@
         jnp.zeros((prompts, rows, H), jnp.float32),
         jnp.zeros((prompts, rows, H, LAT), jnp.float32),
     )
-    piece = lax.all_gather(blended, "group", axis=1, tiled=True)
+    piece = jnp.concatenate(
+        lax.all_to_all(jnp.stack([blended] * lax.axis_size("group")), "group", 0, 0), axis=1
+    )
 
     def one_group(index, carry):
         keys = lax.dynamic_slice_in_dim(piece, index, 1, 1)[:, 0]

time: 242 us -> 207 us (0.86)
  waiting for transfers between devices: 79.4 us -> 42.3 us
  starting transfers between devices: 0.12 us -> 8.3 us
  local copies, waits for them, and re-layouts: 52.4 us -> 45.1 us
    all_gather x1 -> x0, waiting for transfers between devices: 31.9 us -> none  [shards(): piece = lax.all_gather(blended, 'group', axis=1, tiled=True)]
    all_gather x1, waiting for transfers between devices: 46.8 us -> 36.6 us  [whole_of(): whole = lax.all_gather(whole, axes[number], axis=dim, tiled=True)]
    unnamed x18 -> x13, local copies, waits for them, and re-layouts: 11.4 us -> 2.54 us
    all_to_all x0 -> x1, starting transfers between devices: none -> 8.22 us  [shards(): lax.all_to_all(jnp.stack([blended] * lax.axis_size('group')), 'group', 0, 0)]
    all_to_all x0 -> x1, waiting for transfers between devices: none -> 4.99 us  [shards(): lax.all_to_all(jnp.stack([blended] * lax.axis_size('group')), 'group', 0, 0)]
    another operation x2 -> x3, local copies, waits for them, and re-layouts: 0.19 us -> 2.71 us  [the longest x1 2.52 us: shards(): jnp.stack([blended] * lax.axis_size('group'))]
  transfers between devices with their start and end apart: 3 -> 3, of which waited for: 2 -> 2; matrix products, arithmetic and copies ran while one was open for 49% -> 54% of each run, Pallas kernels for 0% -> 0%
where the time goes in v1:
time: 207 us; the launch traced here: 203 us
  matrix products  48.1 us (23%)
  local copies, waits for them, and re-layouts  45.1 us (22%)
  waiting for transfers between devices  42.3 us (20%)
  other arithmetic  23.1 us (11%)
  between operations  14.3 us (7%)
  loops' own time  11.3 us (5%)
  blocking collectives  10.8 us (5%)
  starting transfers between devices  8.3 us (4%)
    all_gather x1, waiting for transfers between devices, whole_of(): whole = lax.all_gather(whole, axes[number], axis=dim, tiled=True)  36.6 us
    dynamic_slice x16, local copies, waits for them, and re-layouts, one_group(): keys = lax.dynamic_slice_in_dim(piece, index, 1, 1)[:, 0]  26.3 us
    dot_general x8, matrix products, update(): jnp.einsum('pqhe,pke->pqhk', query_vec, keys, preferred_element_type=jnp....  20.2 us
    dot_general x8, matrix products, update(): jnp.einsum('pqhk,pkl->pqhl', probs.astype(jnp.bfloat16), keys[..., :LAT],...  17.8 us
    all_gather x1, blocking collectives, whole_of(): whole = lax.all_gather(whole, axes[number], axis=dim, tiled=True)  10.8 us
    another operation x1, loops' own time, shards(): lax.fori_loop(0, piece.shape[1], one_group, start_state)  10.7 us
    all_to_all x1, starting transfers between devices, shards(): lax.all_to_all(jnp.stack([blended] * lax.axis_size('group')), 'group', 0, 0)  8.22 us
    all_gather x1, local copies, waits for them, and re-layouts, whole_of(): whole = lax.all_gather(whole, axes[number], axis=dim, tiled=True)  6.52 us
  transfers between devices with their start and end apart: 3, of which 2 were waited for; matrix products, arithmetic and copies ran while one was open for 54% of the time, Pallas kernels for 0%

profile of v1, /device:TPU:57, one launch (start us, length us, event | category | flops | bytes accessed | tf_op | source)
XLA Modules:
  0.0 203.4 jit_solution(1903891036483067966)
XLA Ops:
  7.2 10.8 %all_gather.9 = bf16[64,4096]{1,0:T(8,128)(2,1)} all-gather(bf16[16,4096]{1,0:T(8,128)(2,1)} %param.18), channel_id=1, replica_groups=mesh['group'=8,'prompt_0'=8,'prompt_1'=4] {'prompt_1'}, dimensions={0}, use_global_device_ids=true | all-gather | bytes 655360 | tf_op jit(solution)/shard_map/all_gather | solution.py:19
  25.8 2.5 %stack.2 = bf16[8,1,1,512,576]{3,4,2,1,0:T(8,128)(2,1)} broadcast(bf16[512,576]{0,1:T(8,128)(2,1)S(1)} %copy.52), dimensions={3,4} | broadcast | bytes 5308416 | tf_op jit(solution)/shard_map/stack | solution.py:93
  28.3 8.2 %all-to-all-start = ((bf16[8,1,1,512,576]{3,4,2,1,0:T(8,128)(2,1)}), bf16[8,1,1,512,576]{3,4,2,1,0:T(8,128)(2,1)}, u32[]{:S(2)}, u32[]{:S(2)}) async-start(bf16[8,1,1,512,576]{3,4,2,1,0:T(8,128)(2,1)} %stack.2), calls=%async_computation | async-start | bytes 9437184 | tf_op jit(solution)/shard_map/all_to_all | solution.py:93
  39.5 36.6 %all-gather.3.cloned.1.call-done = bf16[512,4096]{1,0:T(8,128)(2,1)} async-done(((bf16[64,4096]{1,0:T(8,128)(2,1)}), bf16[512,4096]{1,0:T(8,128)(2,1)}) %all-gather.3.cloned.1.call-update) | async-done | bytes 4194320 | tf_op jit(solution)/shard_map/all_gather | solution.py:19
  76.1 6.5 %copy.53 = bf16[512,4096]{0,1:T(8,128)(2,1)} copy(bf16[512,4096]{1,0:T(8,128)(2,1)} %all-gather.3.cloned.1.call-done) | data formatting | bytes 8388608 | tf_op jit(solution)/shard_map/all_gather | solution.py:19
  86.0 5.0 %all-to-all-done = bf16[8,1,1,512,576]{3,4,2,1,0:T(8,128)(2,1)} async-done(((bf16[8,1,1,512,576]{3,4,2,1,0:T(8,128)(2,1)}), bf16[8,1,1,512,576]{3,4,2,1,0:T(8,128)(2,1)}, u32[]{:S(2)}, u32[]{:S(2)}) %all-to-all-start) | async-done | bytes 4718624 | tf_op jit(solution)/shard_map/all_to_all | solution.py:93
  91.3 96.7 %while.20 = (s32[]{:T(128)}, f32[1,64,16]{1,2,0:T(8,128)S(1)}, f32[1,64,16]{1,2,0:T(8,128)S(1)}, f32[1,64,16,512]{3,2,1,0:T(8,128)S(1)}, s32[1,8]{1,0:T(1,128)S(...) while((s32[]{:T(128)}, f32[1,64,16]{1,2,0:T(8,128)S(1)}, ...), condition=%wide.region_8.9_spmd.clone, body=%wide.region_3.8_spmd.clone.sunk | while | flops 1146129920 | bytes 17670692 | solution.py:103
  94.3 9.0 %conditional.3 = ((f32[1,64,16]{1,2,0:T(8,128)S(1)}, f32[1,64,16]{1,2,0:T(8,128)S(1)}, f32[1,64,16,512]{3,2,1,0:T(8,128)S(1)})) conditional(s32[]{:T(128)} %bitcast.97, (f32[1,64,16]{1,2,0:T(8,128)S(1)}, f32[1,64,16]{1,2,0:T(8,128)S(1)}, f32[1,64,16,512]{3,2,1,0:T(8,128)S(1)}) %tuple.66, (s32[1,512]{1,0:T(1,128)S(1)}, s32[1,1,64]{2,1,0:T(1,128)S(1)}, ...), branch_computations={%region_4.0_spmd, %region_5.7_spmd} | conditional | flops 1146129408 | bytes 17668416 | solution.py:101
  95.6 2.6 %fusion.2 = (f32[64,16]{0,1:T(8,128)S(1)}, f32[512,64,16]{0,1,2:T(8,128)S(1)}) fusion(pred[64,512]{1,0:T(8,128)(4,1)S(1)} %broadcast_compare_fusion, bf16[1,64,16,576]{3,1,2,0:T(8,128)(2,1)} %get-tuple-element.279, bf16[1,1,512,576]{2,3,1,0:T(8,128)(2,1)S(1)} %constant_dynamic-slice_fusion), kind=kOutput, calls=%fused_computation.5 | convolution fusion | flops 605551616 | bytes 3903488 | tf_op jit(solution)/shard_map/while/body/eval_jaxpr/cond/branch_1_fun/pqhe,pke->pqhk/dot_general | solution.py:71
  101.1 2.2 %bitcast_add_fusion = f32[1,64,16,512]{3,2,1,0:T(8,128)S(1)} fusion(f32[1,64,16,512]{3,2,1,0:T(8,128)S(1)} %get-tuple-element.281, bf16[64,16,512]{2,0,1:T(8,128)(2,1)S(1)} %get-tuple-element.353, f32[64,16]{1,0:T(8,128)S(1)} %copy.45, bf16[1,512,576]{2,1,0:T(8,128)(2,1)} %bitcast.98), kind=kOutput, calls=%fused_computation.2 | convolution fusion | flops 537919488 | bytes 5771264 | tf_op jit(solution)/shard_map/while/body/eval_jaxpr/cond/branch_1_fun/pqhk,pkl->pqhl/dot_general | solution.py:79
  106.5 9.0 %conditional.3 = ((f32[1,64,16]{1,2,0:T(8,128)S(1)}, f32[1,64,16]{1,2,0:T(8,128)S(1)}, f32[1,64,16,512]{3,2,1,0:T(8,128)S(1)})) conditional(s32[]{:T(128)} %bitcast.97, (f32[1,64,16]{1,2,0:T(8,128)S(1)}, f32[1,64,16]{1,2,0:T(8,128)S(1)}, f32[1,64,16,512]{3,2,1,0:T(8,128)S(1)}) %tuple.66, (s32[1,512]{1,0:T(1,128)S(1)}, s32[1,1,64]{2,1,0:T(1,128)S(1)}, ...), branch_computations={%region_4.0_spmd, %region_5.7_spmd} | conditional | flops 1146129408 | bytes 17668416 | solution.py:101
  107.7 2.5 %fusion.2 = (f32[64,16]{0,1:T(8,128)S(1)}, f32[512,64,16]{0,1,2:T(8,128)S(1)}) fusion(pred[64,512]{1,0:T(8,128)(4,1)S(1)} %broadcast_compare_fusion, bf16[1,64,16,576]{3,1,2,0:T(8,128)(2,1)} %get-tuple-element.279, bf16[1,1,512,576]{2,3,1,0:T(8,128)(2,1)S(1)} %constant_dynamic-slice_fusion), kind=kOutput, calls=%fused_computation.5 | convolution fusion | flops 605551616 | bytes 3903488 | tf_op jit(solution)/shard_map/while/body/eval_jaxpr/cond/branch_1_fun/pqhe,pke->pqhk/dot_general | solution.py:71
  113.2 2.2 %bitcast_add_fusion = f32[1,64,16,512]{3,2,1,0:T(8,128)S(1)} fusion(f32[1,64,16,512]{3,2,1,0:T(8,128)S(1)} %get-tuple-element.281, bf16[64,16,512]{2,0,1:T(8,128)(2,1)S(1)} %get-tuple-element.353, f32[64,16]{1,0:T(8,128)S(1)} %copy.45, bf16[1,512,576]{2,1,0:T(8,128)(2,1)} %bitcast.98), kind=kOutput, calls=%fused_computation.2 | convolution fusion | flops 537919488 | bytes 5771264 | tf_op jit(solution)/shard_map/while/body/eval_jaxpr/cond/branch_1_fun/pqhk,pkl->pqhl/dot_general | solution.py:79
  118.5 9.0 %conditional.3 = ((f32[1,64,16]{1,2,0:T(8,128)S(1)}, f32[1,64,16]{1,2,0:T(8,128)S(1)}, f32[1,64,16,512]{3,2,1,0:T(8,128)S(1)})) conditional(s32[]{:T(128)} %bitcast.97, (f32[1,64,16]{1,2,0:T(8,128)S(1)}, f32[1,64,16]{1,2,0:T(8,128)S(1)}, f32[1,64,16,512]{3,2,1,0:T(8,128)S(1)}) %tuple.66, (s32[1,512]{1,0:T(1,128)S(1)}, s32[1,1,64]{2,1,0:T(1,128)S(1)}, ...), branch_computations={%region_4.0_spmd, %region_5.7_spmd} | conditional | flops 1146129408 | bytes 17668416 | solution.py:101
  119.8 2.5 %fusion.2 = (f32[64,16]{0,1:T(8,128)S(1)}, f32[512,64,16]{0,1,2:T(8,128)S(1)}) fusion(pred[64,512]{1,0:T(8,128)(4,1)S(1)} %broadcast_compare_fusion, bf16[1,64,16,576]{3,1,2,0:T(8,128)(2,1)} %get-tuple-element.279, bf16[1,1,512,576]{2,3,1,0:T(8,128)(2,1)S(1)} %constant_dynamic-slice_fusion), kind=kOutput, calls=%fused_computation.5 | convolution fusion | flops 605551616 | bytes 3903488 | tf_op jit(solution)/shard_map/while/body/eval_jaxpr/cond/branch_1_fun/pqhe,pke->pqhk/dot_general | solution.py:71
  125.3 2.2 %bitcast_add_fusion = f32[1,64,16,512]{3,2,1,0:T(8,128)S(1)} fusion(f32[1,64,16,512]{3,2,1,0:T(8,128)S(1)} %get-tuple-element.281, bf16[64,16,512]{2,0,1:T(8,128)(2,1)S(1)} %get-tuple-element.353, f32[64,16]{1,0:T(8,128)S(1)} %copy.45, bf16[1,512,576]{2,1,0:T(8,128)(2,1)} %bitcast.98), kind=kOutput, calls=%fused_computation.2 | convolution fusion | flops 537919488 | bytes 5771264 | tf_op jit(solution)/shard_map/while/body/eval_jaxpr/cond/branch_1_fun/pqhk,pkl->pqhl/dot_general | solution.py:79
  130.6 9.1 %conditional.3 = ((f32[1,64,16]{1,2,0:T(8,128)S(1)}, f32[1,64,16]{1,2,0:T(8,128)S(1)}, f32[1,64,16,512]{3,2,1,0:T(8,128)S(1)})) conditional(s32[]{:T(128)} %bitcast.97, (f32[1,64,16]{1,2,0:T(8,128)S(1)}, f32[1,64,16]{1,2,0:T(8,128)S(1)}, f32[1,64,16,512]{3,2,1,0:T(8,128)S(1)}) %tuple.66, (s32[1,512]{1,0:T(1,128)S(1)}, s32[1,1,64]{2,1,0:T(1,128)S(1)}, ...), branch_computations={%region_4.0_spmd, %region_5.7_spmd} | conditional | flops 1146129408 | bytes 17668416 | solution.py:101
  131.9 2.5 %fusion.2 = (f32[64,16]{0,1:T(8,128)S(1)}, f32[512,64,16]{0,1,2:T(8,128)S(1)}) fusion(pred[64,512]{1,0:T(8,128)(4,1)S(1)} %broadcast_compare_fusion, bf16[1,64,16,576]{3,1,2,0:T(8,128)(2,1)} %get-tuple-element.279, bf16[1,1,512,576]{2,3,1,0:T(8,128)(2,1)S(1)} %constant_dynamic-slice_fusion), kind=kOutput, calls=%fused_computation.5 | convolution fusion | flops 605551616 | bytes 3903488 | tf_op jit(solution)/shard_map/while/body/eval_jaxpr/cond/branch_1_fun/pqhe,pke->pqhk/dot_general | solution.py:71
  137.4 2.2 %bitcast_add_fusion = f32[1,64,16,512]{3,2,1,0:T(8,128)S(1)} fusion(f32[1,64,16,512]{3,2,1,0:T(8,128)S(1)} %get-tuple-element.281, bf16[64,16,512]{2,0,1:T(8,128)(2,1)S(1)} %get-tuple-element.353, f32[64,16]{1,0:T(8,128)S(1)} %copy.45, bf16[1,512,576]{2,1,0:T(8,128)(2,1)} %bitcast.98), kind=kOutput, calls=%fused_computation.2 | convolution fusion | flops 537919488 | bytes 5771264 | tf_op jit(solution)/shard_map/while/body/eval_jaxpr/cond/branch_1_fun/pqhk,pkl->pqhl/dot_general | solution.py:79
  142.7 9.1 %conditional.3 = ((f32[1,64,16]{1,2,0:T(8,128)S(1)}, f32[1,64,16]{1,2,0:T(8,128)S(1)}, f32[1,64,16,512]{3,2,1,0:T(8,128)S(1)})) conditional(s32[]{:T(128)} %bitcast.97, (f32[1,64,16]{1,2,0:T(8,128)S(1)}, f32[1,64,16]{1,2,0:T(8,128)S(1)}, f32[1,64,16,512]{3,2,1,0:T(8,128)S(1)}) %tuple.66, (s32[1,512]{1,0:T(1,128)S(1)}, s32[1,1,64]{2,1,0:T(1,128)S(1)}, ...), branch_computations={%region_4.0_spmd, %region_5.7_spmd} | conditional | flops 1146129408 | bytes 17668416 | solution.py:101
  144.0 2.5 %fusion.2 = (f32[64,16]{0,1:T(8,128)S(1)}, f32[512,64,16]{0,1,2:T(8,128)S(1)}) fusion(pred[64,512]{1,0:T(8,128)(4,1)S(1)} %broadcast_compare_fusion, bf16[1,64,16,576]{3,1,2,0:T(8,128)(2,1)} %get-tuple-element.279, bf16[1,1,512,576]{2,3,1,0:T(8,128)(2,1)S(1)} %constant_dynamic-slice_fusion), kind=kOutput, calls=%fused_computation.5 | convolution fusion | flops 605551616 | bytes 3903488 | tf_op jit(solution)/shard_map/while/body/eval_jaxpr/cond/branch_1_fun/pqhe,pke->pqhk/dot_general | solution.py:71
  149.5 2.2 %bitcast_add_fusion = f32[1,64,16,512]{3,2,1,0:T(8,128)S(1)} fusion(f32[1,64,16,512]{3,2,1,0:T(8,128)S(1)} %get-tuple-element.281, bf16[64,16,512]{2,0,1:T(8,128)(2,1)S(1)} %get-tuple-element.353, f32[64,16]{1,0:T(8,128)S(1)} %copy.45, bf16[1,512,576]{2,1,0:T(8,128)(2,1)} %bitcast.98), kind=kOutput, calls=%fused_computation.2 | convolution fusion | flops 537919488 | bytes 5771264 | tf_op jit(solution)/shard_map/while/body/eval_jaxpr/cond/branch_1_fun/pqhk,pkl->pqhl/dot_general | solution.py:79
  154.9 9.0 %conditional.3 = ((f32[1,64,16]{1,2,0:T(8,128)S(1)}, f32[1,64,16]{1,2,0:T(8,128)S(1)}, f32[1,64,16,512]{3,2,1,0:T(8,128)S(1)})) conditional(s32[]{:T(128)} %bitcast.97, (f32[1,64,16]{1,2,0:T(8,128)S(1)}, f32[1,64,16]{1,2,0:T(8,128)S(1)}, f32[1,64,16,512]{3,2,1,0:T(8,128)S(1)}) %tuple.66, (s32[1,512]{1,0:T(1,128)S(1)}, s32[1,1,64]{2,1,0:T(1,128)S(1)}, ...), branch_computations={%region_4.0_spmd, %region_5.7_spmd} | conditional | flops 1146129408 | bytes 17668416 | solution.py:101
  156.1 2.5 %fusion.2 = (f32[64,16]{0,1:T(8,128)S(1)}, f32[512,64,16]{0,1,2:T(8,128)S(1)}) fusion(pred[64,512]{1,0:T(8,128)(4,1)S(1)} %broadcast_compare_fusion, bf16[1,64,16,576]{3,1,2,0:T(8,128)(2,1)} %get-tuple-element.279, bf16[1,1,512,576]{2,3,1,0:T(8,128)(2,1)S(1)} %constant_dynamic-slice_fusion), kind=kOutput, calls=%fused_computation.5 | convolution fusion | flops 605551616 | bytes 3903488 | tf_op jit(solution)/shard_map/while/body/eval_jaxpr/cond/branch_1_fun/pqhe,pke->pqhk/dot_general | solution.py:71
  161.6 2.2 %bitcast_add_fusion = f32[1,64,16,512]{3,2,1,0:T(8,128)S(1)} fusion(f32[1,64,16,512]{3,2,1,0:T(8,128)S(1)} %get-tuple-element.281, bf16[64,16,512]{2,0,1:T(8,128)(2,1)S(1)} %get-tuple-element.353, f32[64,16]{1,0:T(8,128)S(1)} %copy.45, bf16[1,512,576]{2,1,0:T(8,128)(2,1)} %bitcast.98), kind=kOutput, calls=%fused_computation.2 | convolution fusion | flops 537919488 | bytes 5771264 | tf_op jit(solution)/shard_map/while/body/eval_jaxpr/cond/branch_1_fun/pqhk,pkl->pqhl/dot_general | solution.py:79
  166.9 9.0 %conditional.3 = ((f32[1,64,16]{1,2,0:T(8,128)S(1)}, f32[1,64,16]{1,2,0:T(8,128)S(1)}, f32[1,64,16,512]{3,2,1,0:T(8,128)S(1)})) conditional(s32[]{:T(128)} %bitcast.97, (f32[1,64,16]{1,2,0:T(8,128)S(1)}, f32[1,64,16]{1,2,0:T(8,128)S(1)}, f32[1,64,16,512]{3,2,1,0:T(8,128)S(1)}) %tuple.66, (s32[1,512]{1,0:T(1,128)S(1)}, s32[1,1,64]{2,1,0:T(1,128)S(1)}, ...), branch_computations={%region_4.0_spmd, %region_5.7_spmd} | conditional | flops 1146129408 | bytes 17668416 | solution.py:101
  168.2 2.5 %fusion.2 = (f32[64,16]{0,1:T(8,128)S(1)}, f32[512,64,16]{0,1,2:T(8,128)S(1)}) fusion(pred[64,512]{1,0:T(8,128)(4,1)S(1)} %broadcast_compare_fusion, bf16[1,64,16,576]{3,1,2,0:T(8,128)(2,1)} %get-tuple-element.279, bf16[1,1,512,576]{2,3,1,0:T(8,128)(2,1)S(1)} %constant_dynamic-slice_fusion), kind=kOutput, calls=%fused_computation.5 | convolution fusion | flops 605551616 | bytes 3903488 | tf_op jit(solution)/shard_map/while/body/eval_jaxpr/cond/branch_1_fun/pqhe,pke->pqhk/dot_general | solution.py:71
  173.7 2.2 %bitcast_add_fusion = f32[1,64,16,512]{3,2,1,0:T(8,128)S(1)} fusion(f32[1,64,16,512]{3,2,1,0:T(8,128)S(1)} %get-tuple-element.281, bf16[64,16,512]{2,0,1:T(8,128)(2,1)S(1)} %get-tuple-element.353, f32[64,16]{1,0:T(8,128)S(1)} %copy.45, bf16[1,512,576]{2,1,0:T(8,128)(2,1)} %bitcast.98), kind=kOutput, calls=%fused_computation.2 | convolution fusion | flops 537919488 | bytes 5771264 | tf_op jit(solution)/shard_map/while/body/eval_jaxpr/cond/branch_1_fun/pqhk,pkl->pqhl/dot_general | solution.py:79
  179.0 9.0 %conditional.3 = ((f32[1,64,16]{1,2,0:T(8,128)S(1)}, f32[1,64,16]{1,2,0:T(8,128)S(1)}, f32[1,64,16,512]{3,2,1,0:T(8,128)S(1)})) conditional(s32[]{:T(128)} %bitcast.97, (f32[1,64,16]{1,2,0:T(8,128)S(1)}, f32[1,64,16]{1,2,0:T(8,128)S(1)}, f32[1,64,16,512]{3,2,1,0:T(8,128)S(1)}) %tuple.66, (s32[1,512]{1,0:T(1,128)S(1)}, s32[1,1,64]{2,1,0:T(1,128)S(1)}, ...), branch_computations={%region_4.0_spmd, %region_5.7_spmd} | conditional | flops 1146129408 | bytes 17668416 | solution.py:101
  180.2 2.5 %fusion.2 = (f32[64,16]{0,1:T(8,128)S(1)}, f32[512,64,16]{0,1,2:T(8,128)S(1)}) fusion(pred[64,512]{1,0:T(8,128)(4,1)S(1)} %broadcast_compare_fusion, bf16[1,64,16,576]{3,1,2,0:T(8,128)(2,1)} %get-tuple-element.279, bf16[1,1,512,576]{2,3,1,0:T(8,128)(2,1)S(1)} %constant_dynamic-slice_fusion), kind=kOutput, calls=%fused_computation.5 | convolution fusion | flops 605551616 | bytes 3903488 | tf_op jit(solution)/shard_map/while/body/eval_jaxpr/cond/branch_1_fun/pqhe,pke->pqhk/dot_general | solution.py:71
  188.3 2.4 %fusion.26 = bf16[1,64,16,128]{3,1,2,0:T(8,128)(2,1)S(1)} fusion(bf16[512,16,256]{0,2,1:T(8,128)(2,1)} %bitcast.100, bf16[64,16,512]{2,1,0:T(8,128)(2,1)S(1)} %fusion.30), kind=kOutput, calls=%fused_computation.34 | convolution fusion | flops 134348800 | bytes 3407872 | tf_op jit(solution)/shard_map/pqhl,lhv->pqhv/dot_general | solution.py:105
  190.9 5.7 %fusion.12 = bf16[1,1,64,2048]{3,2,1,0:T(8,128)(2,1)} fusion(bf16[2048,2048]{1,0:T(8,128)(2,1)} %all-gather.5.cloned.1.call-done, bf16[8,8,16,128]{3,2,1,0:T(8,128)(2,1)S(1)} %bitcast.104), kind=kOutput, calls=%fused_computation.24 | convolution fusion | flops 537001984 | bytes 8912896 | tf_op jit(solution)/shard_map/dot_general | solution.py:110
  (155 shorter events, 64.3 us)
Async XLA Ops:
  7.2 16.8 %copy-start.3 = (bf16[1,1,64,576]{3,2,1,0:T(8,128)(2,1)S(1)}, bf16[1,1,64,576]{3,2,1,0:T(8,128)(2,1)}, u32[]{:S(2)}) copy-start(bf16[1,1,64,576]{3,2,1,0:T(8,128)(2,1)} %param.13) | copy-start | bytes 221188
  7.2 16.8 %copy-start.4 = (bf16[512]{0:T(512)(128)(2,1)S(1)}, bf16[512]{0:T(512)(128)(2,1)}, u32[]{:S(2)}) copy-start(bf16[512]{0:T(512)(128)(2,1)} %param.17) | copy-start | bytes 3076
  7.2 68.9 %all-gather.3.cloned.1.call-start = ((), (), s32[]{:S(2)}) async-start(), calls=%async_computation.1 | async-start | bytes 4718592 | tf_op jit(solution)/shard_map/all_gather | solution.py:19
  18.1 172.8 %all-gather.5.cloned.1.call-start = ((), (), s32[]{:S(2)}) async-start(), calls=%async_computation.2 | async-start | bytes 8650752 | tf_op jit(solution)/shard_map/all_gather | solution.py:109
  28.3 8.2 %copy-start.2 = (bf16[1,1,64,3072]{3,2,1,0:T(8,128)(2,1)S(1)}, bf16[1,1,64,3072]{3,2,1,0:T(8,128)(2,1)}, u32[]{:S(2)}) copy-start(bf16[1,1,64,3072]{3,2,1,0:T(8,128)(2,1)} %param.12) | copy-start | bytes 1179652
  28.3 62.6 %all-to-all-start = ((bf16[8,1,1,512,576]{3,4,2,1,0:T(8,128)(2,1)}), bf16[8,1,1,512,576]{3,4,2,1,0:T(8,128)(2,1)}, u32[]{:S(2)}, u32[]{:S(2)}) async-start(bf16[8,1,1,512,576]{3,4,2,1,0:T(8,128)(2,1)} %stack.2), calls=%async_computation | async-start | bytes 9437184 | tf_op jit(solution)/shard_map/all_to_all | solution.py:93
  37.2 2.4 %copy-start.1 = (bf16[1,1,64,16,192]{4,3,2,1,0:T(8,128)(2,1)}, bf16[1,1,64,16,192]{4,3,2,1,0:T(8,128)(2,1)S(1)}, u32[]{:S(2)}) copy-start(bf16[1,1,64,16,192]{4,3,2,1,0:T(8,128)(2,1)S(1)} %reshape.425) | copy-start | bytes 1179652
  76.1 6.5 %slice-start = ((bf16[1,1,64,16,192]{4,3,2,1,0:T(8,128)(2,1)}), bf16[1,1,64,16,128]{4,3,2,1,0:T(8,128)(2,1)S(1)}, s32[]{:S(2)}) async-start(bf16[1,1,64,16,192]{4,3,2,1,0:T(8,128)(2,1)} %copy-done.1), calls=%async_computation.3 | async-start | bytes 524288 | tf_op jit(solution)/shard_map/slice | solution.py:56
  84.6 6.6 %copy-start.5 = (s32[1,8]{1,0:T(1,128)S(1)}, s32[1,8]{1,0:T(1,128)}, u32[]{:S(2)}) copy-start(s32[1,8]{1,0:T(1,128)} %param.16) | copy-start | bytes 100
  95.5 2.7 %copy-start = (bf16[1,1,512,576]{2,3,1,0:T(8,128)(2,1)}, bf16[1,1,512,576]{2,3,1,0:T(8,128)(2,1)S(1)}, u32[]{:S(2)}) copy-start(bf16[1,1,512,576]{2,3,1,0:T(8,128)(2,1)S(1)} %constant_dynamic-slice_fusion) | copy-start | bytes 1769476 | tf_op jit(solution)/shard_map/while/body/eval_jaxpr/cond
  107.6 2.6 %copy-start = (bf16[1,1,512,576]{2,3,1,0:T(8,128)(2,1)}, bf16[1,1,512,576]{2,3,1,0:T(8,128)(2,1)S(1)}, u32[]{:S(2)}) copy-start(bf16[1,1,512,576]{2,3,1,0:T(8,128)(2,1)S(1)} %constant_dynamic-slice_fusion) | copy-start | bytes 1769476 | tf_op jit(solution)/shard_map/while/body/eval_jaxpr/cond
  119.7 2.6 %copy-start = (bf16[1,1,512,576]{2,3,1,0:T(8,128)(2,1)}, bf16[1,1,512,576]{2,3,1,0:T(8,128)(2,1)S(1)}, u32[]{:S(2)}) copy-start(bf16[1,1,512,576]{2,3,1,0:T(8,128)(2,1)S(1)} %constant_dynamic-slice_fusion) | copy-start | bytes 1769476 | tf_op jit(solution)/shard_map/while/body/eval_jaxpr/cond
  131.8 2.6 %copy-start = (bf16[1,1,512,576]{2,3,1,0:T(8,128)(2,1)}, bf16[1,1,512,576]{2,3,1,0:T(8,128)(2,1)S(1)}, u32[]{:S(2)}) copy-start(bf16[1,1,512,576]{2,3,1,0:T(8,128)(2,1)S(1)} %constant_dynamic-slice_fusion) | copy-start | bytes 1769476 | tf_op jit(solution)/shard_map/while/body/eval_jaxpr/cond
  143.9 2.6 %copy-start = (bf16[1,1,512,576]{2,3,1,0:T(8,128)(2,1)}, bf16[1,1,512,576]{2,3,1,0:T(8,128)(2,1)S(1)}, u32[]{:S(2)}) copy-start(bf16[1,1,512,576]{2,3,1,0:T(8,128)(2,1)S(1)} %constant_dynamic-slice_fusion) | copy-start | bytes 1769476 | tf_op jit(solution)/shard_map/while/body/eval_jaxpr/cond
  156.0 2.6 %copy-start = (bf16[1,1,512,576]{2,3,1,0:T(8,128)(2,1)}, bf16[1,1,512,576]{2,3,1,0:T(8,128)(2,1)S(1)}, u32[]{:S(2)}) copy-start(bf16[1,1,512,576]{2,3,1,0:T(8,128)(2,1)S(1)} %constant_dynamic-slice_fusion) | copy-start | bytes 1769476 | tf_op jit(solution)/shard_map/while/body/eval_jaxpr/cond
  168.1 2.6 %copy-start = (bf16[1,1,512,576]{2,3,1,0:T(8,128)(2,1)}, bf16[1,1,512,576]{2,3,1,0:T(8,128)(2,1)S(1)}, u32[]{:S(2)}) copy-start(bf16[1,1,512,576]{2,3,1,0:T(8,128)(2,1)S(1)} %constant_dynamic-slice_fusion) | copy-start | bytes 1769476 | tf_op jit(solution)/shard_map/while/body/eval_jaxpr/cond
  180.1 2.6 %copy-start = (bf16[1,1,512,576]{2,3,1,0:T(8,128)(2,1)}, bf16[1,1,512,576]{2,3,1,0:T(8,128)(2,1)S(1)}, u32[]{:S(2)}) copy-start(bf16[1,1,512,576]{2,3,1,0:T(8,128)(2,1)S(1)} %constant_dynamic-slice_fusion) | copy-start | bytes 1769476 | tf_op jit(solution)/shard_map/while/body/eval_jaxpr/cond
Sparse Core Ops, SparseCore 0:
  18.2 57.8 all-gather.2
  78.7 94.4 all-gather.4
